TPU v7x, 32 devices: a whole 2x2x4 slice. The times are simulated.
32 devices in a mesh: gx: 16 (over z, x, core), gy: 2 (over y).
Axes of the slice: x: 2, y: 2, z: 4, core: 2. Of those that a mesh axis runs over, the one named last changes fastest.
Arguments:
- queries: bfloat16 [64, 128, 1024], P('gx', 'gy'), may hold values from -42 to 42
- key_tokens: bfloat16 [64, 128, 1024], P('gx', 'gy'), may hold values from -6 to 6
- value_tokens: bfloat16 [64, 128, 1024], P('gx', 'gy'), may hold values from -6 to 6
- out_grad: bfloat16 [64, 128, 1024], P('gx', 'gy'), may hold values from -6 to 6
- conv_weight: float32 [9, 1024], replicated, may hold values from -0.9 to 0.9
- block_pairs: int32 [16, 2, 16, 2], P('gx', 'gy'), may hold values from 0 to 31, as said below
Outputs:
- layer_out: bfloat16 [64, 128, 1024], P('gx', 'gy')
- query_grad: bfloat16 [64, 128, 1024], P('gx', 'gy')
- key_grad: bfloat16 [64, 128, 1024], P('gx', 'gy')
- value_grad: bfloat16 [64, 128, 1024], P('gx', 'gy')
Inputs may be any that keep to these rules, and one draw needn't show every extreme that they name: block_pairs[i, j, p] = (a local query block of tile (i, j), below 2; a key block of column j, which lies on tile (key block) // 2 along the first dimension). That tile is i + o modulo 16 with o one of 0, 1, -1, 4, 8, 12. Pairs may repeat.
All inputs are finite; a program needn't handle non-finite values.
Results may differ from a plain program's by a relative error of at most 0.009.
Values may be sent and summed in bfloat16 or wider, within the bound.
A program may use at most 128 MiB of HBM per device.

v0:
```python
import functools
import math

import jax
import jax.numpy as jnp
from jax import lax
from jax.experimental import pallas as pl
from jax.experimental.pallas import tpu as pltpu
from jax.sharding import PartitionSpec as P

HD = 128
BLOCK = 128
NEG = -1e30
MESH = pl.DeviceIdType.MESH
SCALE = 1.0 / math.sqrt(HD)
LOG2E = math.log2(math.e)
F32 = jnp.float32
BF16 = jnp.bfloat16


def kernel(
    n, m, tx, ty,
    q_ref, k_ref, v_ref, g_ref, w_ref, bias_ref,
    o_ref, dq_ref, dk_ref, dv_ref,
    qg, gg, kk, vv, bias_g, s_sc, dk_acc, dv_acc,
    part_send, part_recv, res, ret, edge, slab, conv,
    send_sem, recv_sem, local_sem,
):
    tokens = tx * ty
    heads = q_ref.shape[2] // HD
    hp = heads // 4
    quarter = n // 4
    own = lax.axis_index("gx")
    col = lax.axis_index("gy")
    slot = own // quarter
    rank = lax.rem(own, quarter)

    def far(d):
        return {"gx": lax.rem(own + d * quarter, n)}

    next_group = {"gx": slot * quarter + lax.rem(rank + 1, quarter)}
    prev_group = {"gx": slot * quarter + lax.rem(rank + quarter - 1, quarter)}
    next_tile = {"gx": lax.rem(own + 1, n)}
    prev_tile = {"gx": lax.rem(own + n - 1, n)}
    next_col = {"gy": lax.rem(col + 1, m)}
    prev_col = {"gy": lax.rem(col + m - 1, m)}

    barrier = pltpu.get_barrier_semaphore()
    partners = [far(1), far(2), far(3), next_group, prev_group, next_tile, prev_tile, next_col, prev_col]
    for partner in partners:
        pl.semaphore_signal(barrier, inc=1, device_id=partner, device_id_type=MESH)
    pl.semaphore_wait(barrier, len(partners))

    count = [0]
    sent = []

    def send(src, dst, device):
        at = count[0]
        count[0] += 1
        copy = pltpu.make_async_remote_copy(
            src_ref=src, dst_ref=dst, send_sem=send_sem.at[at], recv_sem=recv_sem.at[at],
            device_id=device, device_id_type=MESH,
        )
        copy.start()
        sent.append(copy)
        return copy

    edge_copies = []

    def edge_send(src, dst, device, sends, receives):
        at = count[0]
        count[0] += 1
        copy = pltpu.make_async_remote_copy(
            src_ref=src, dst_ref=dst, send_sem=send_sem.at[at], recv_sem=recv_sem.at[at],
            device_id=device, device_id_type=MESH,
        )

        @pl.when(sends)
        def _():
            copy.start()

        @pl.when(jnp.logical_not(receives))
        def _():
            dst[...] = jnp.zeros(dst.shape, BF16)

        edge_copies.append((copy, sends, receives))

    def head_cols(head):
        return pl.ds(pl.multiple_of(head * HD, HD), HD)

    order = (2, 1, 3)
    arrays = ((k_ref, lambda h, s: kk.at[h, 0, s]), (v_ref, lambda h, s: vv.at[h, 0, s]),
              (q_ref, lambda h, s: qg.at[h, s]), (g_ref, lambda h, s: gg.at[h, s]))
    incoming = {}
    locals_ = []
    for h in range(hp):
        for a, (ref, place) in enumerate(arrays):
            for d in order:
                target = lax.rem(slot + d, 4)
                incoming[h, a, d] = send(ref.at[:, :, head_cols(target * hp + h)], place(h, slot), far(d))
            mine = pltpu.make_async_copy(
                ref.at[:, :, head_cols(slot * hp + h)], place(h, slot), local_sem.at[h * 4 + a])
            mine.start()
            locals_.append(mine)
        if h == 0:
            for a, ref in enumerate((v_ref, g_ref)):
                edge_send(ref.at[pl.ds(tx - 1, 1)], edge.at[a, pl.ds(0, 1)], next_tile, own < n - 1, own > 0)
                edge_send(ref.at[pl.ds(0, 1)], edge.at[a, pl.ds(1, 1)], prev_tile, own > 0, own < n - 1)
            bias_copies = [send(bias_ref, bias_g.at[slot], far(d)) for d in order]
            mine = pltpu.make_async_copy(bias_ref, bias_g.at[slot], local_sem.at[hp * 4])
            mine.start()
            locals_.append(mine)
    slab_copies = []
    for a, ref in enumerate((v_ref, g_ref)):
        slab_copies.append(send(ref.at[:, pl.ds(ty - 16, 16)], slab.at[a, 0, pl.ds(1, tx)], next_col))
        slab_copies.append(send(ref.at[:, pl.ds(0, 16)], slab.at[a, 1, pl.ds(1, tx)], prev_col))
    for mine in locals_:
        mine.wait()

    forwards = {}

    def forward(h, d):
        s = lax.rem(slot + 4 - d, 4)
        for a, buf in enumerate((kk, vv)):
            if d:
                incoming[h, a, d].wait_recv()
            forwards[h, a, d, 1] = send(buf.at[h, 0, s], buf.at[h, 1, s], prev_group)
            forwards[h, a, d, 2] = send(buf.at[h, 0, s], buf.at[h, 2, s], next_group)

    for h in range(hp):
        forward(h, 0)
    for copy, _, receives in edge_copies:
        pl.when(receives)(copy.wait_recv)
    for a in range(2):
        for x, e in ((0, 0), (tx + 1, 1)):
            slab_copies.append(send(edge.at[a, pl.ds(e, 1), pl.ds(ty - 16, 16)], slab.at[a, 0, pl.ds(x, 1)], next_col))
            slab_copies.append(send(edge.at[a, pl.ds(e, 1), pl.ds(0, 16)], slab.at[a, 1, pl.ds(x, 1)], prev_col))
    for d in (1, 3, 2):
        forward(0, d)

    for copy in slab_copies:
        copy.wait_recv()
    has_up = (own > 0).astype(F32)
    has_down = (own < n - 1).astype(F32)
    has_left = (col > 0).astype(F32)
    has_right = (col < m - 1).astype(F32)
    for a, ref in enumerate((v_ref, g_ref)):

        @pl.loop(0, heads)
        def _(c, a=a, ref=ref):
            cols = head_cols(c)
            row_id = lax.broadcasted_iota(jnp.int32, (ty, HD), 0)
            sums = [None] * tx
            for x in range(tx + 2):
                if x == 0:
                    row = edge[a, 0, :, cols].astype(F32) * has_up
                elif x == tx + 1:
                    row = edge[a, 1, :, cols].astype(F32) * has_down
                else:
                    row = ref[x - 1, :, cols].astype(F32)
                left = slab[a, 0, x, :, cols].astype(F32)[15:16] * has_left
                right = slab[a, 1, x, :, cols].astype(F32)[0:1] * has_right
                if x == 0:
                    left, right = left * has_up, right * has_up
                if x == tx + 1:
                    left, right = left * has_down, right * has_down
                shifted = (
                    jnp.where(row_id == 0, left, pltpu.roll(row, 1, 0)),
                    row,
                    jnp.where(row_id == ty - 1, right, pltpu.roll(row, ty - 1, 0)),
                )
                for step in (-1, 0, 1):
                    target = x - 1 - step
                    if 0 <= target < tx:
                        for b in range(3):
                            tap = 3 * (step + 1) + b
                            tap = tap if a == 0 else 8 - tap
                            term = w_ref[pl.ds(tap, 1), cols] * shifted[b]
                            sums[target] = term if sums[target] is None else sums[target] + term
            for x in range(tx):
                conv[a, x, :, cols] = sums[x]

    for h in range(1, hp):
        for d in (1, 3, 2):
            forward(h, d)
    for copy in bias_copies:
        copy.wait_recv()

    ahead = (rank == quarter - 1).astype(jnp.int32)
    behind = 3 * (rank == 0).astype(jnp.int32)
    nt = (((1,), (1,)), ((), ()))
    nn = (((1,), (0,)), ((), ()))
    tn = (((0,), (0,)), ((), ()))

    def dot(x, y, dims):
        return lax.dot_general(x, y, dims, preferred_element_type=F32)

    def flat(x):
        return x.reshape(tokens, HD)

    def attend(h):
        dk_acc[h] = jnp.zeros(dk_acc.shape[1:], F32)
        dv_acc[h] = jnp.zeros(dv_acc.shape[1:], F32)

        @pl.loop(0, 4)
        def _(i):
            q = flat(qg[h, i])
            g = flat(gg[h, i])
            keys = [(0, 0), (0, 1), (0, 2), (0, 3), (1, lax.rem(i + ahead, 4)), (2, lax.rem(i + behind, 4))]
            top = None
            for j, (nb, s) in enumerate(keys):
                js = pl.ds(j * tokens, tokens)
                score = dot(q, flat(kk[h, nb, s]), nt)
                bias = bias_g[i, :, js]
                parts = [score[b * BLOCK:(b + 1) * BLOCK] + bias[b:b + 1] for b in range(tokens // BLOCK)]
                score = jnp.concatenate(parts, axis=0)
                s_sc[:, js] = score
                peak = jnp.max(score, axis=1, keepdims=True)
                top = peak if top is None else jnp.maximum(top, peak)
            total = jnp.zeros((tokens, 1), F32)
            out = jnp.zeros((tokens, HD), F32)
            for j, (nb, s) in enumerate(keys):
                js = pl.ds(j * tokens, tokens)
                prob = jnp.exp2((s_sc[:, js] - top) * (SCALE * LOG2E))
                s_sc[:, js] = prob
                total = total + jnp.sum(prob, axis=1, keepdims=True)
                out = out + dot(prob.astype(BF16), flat(vv[h, nb, s]), nn)
            inv = 1.0 / total
            out = out * inv
            res[0, h, i] = out.astype(BF16).reshape(tx, ty, HD)
            grad_dot = jnp.sum(g.astype(F32) * out, axis=1, keepdims=True)
            dq = jnp.zeros((tokens, HD), F32)
            for j, (nb, s) in enumerate(keys):
                js = pl.ds(j * tokens, tokens)
                prob_grad = dot(g, flat(vv[h, nb, s]), nt)
                prob = s_sc[:, js] * inv
                score_grad = (prob * (prob_grad - grad_dot)).astype(BF16)
                dq = dq + dot(score_grad, flat(kk[h, nb, s]), nn)
                dk = dot(score_grad, q, tn)
                dv = dot(prob.astype(BF16), g, tn)
                if nb == 0:
                    dk_acc[h, s] += dk
                    dv_acc[h, s] += dv
                else:
                    part_send[0, h, nb - 1, s] = dk.astype(BF16).reshape(tx, ty, HD)
                    part_send[1, h, nb - 1, s] = dv.astype(BF16).reshape(tx, ty, HD)
            res[1, h, i] = (dq * SCALE).astype(BF16).reshape(tx, ty, HD)

    back = {0: [], 1: [], 2: [], 3: []}

    def give_back(a, h):
        for d in order:
            target = lax.rem(slot + d, 4)
            back[a].append(send(res.at[a, h, target], ret.at[a, slot * hp + h], far(d)))

    parts = {}

    def work(h):
        for d in order:
            for a in (2, 3):
                incoming[h, a, d].wait_recv()
        for a in range(2):
            for d in range(4):
                for nb in (1, 2):
                    forwards[h, a, d, nb].wait_recv()
        if h:
            finish(h - 1)
        attend(h)
        parts[h] = [
            send(part_send.at[a, h, nb], part_recv.at[a, h, nb], (next_group, prev_group)[nb])
            for a in range(2) for nb in range(2)
        ]
        for a in (0, 1):
            give_back(a, h)

    def finish(h):
        for copy in parts[h]:
            copy.wait_recv()
        for a, acc in enumerate((dk_acc, dv_acc)):
            for s in range(4):
                value = acc[h, s] + flat(part_recv[a, h, 0, s]).astype(F32) + flat(part_recv[a, h, 1, s]).astype(F32)
                if a == 0:
                    value = value * SCALE
                res[2 + a, h, s] = value.astype(BF16).reshape(tx, ty, HD)
            give_back(2 + a, h)

    for h in range(hp):
        work(h)
    finish(hp - 1)
    outputs = (o_ref, dq_ref, dk_ref, dv_ref)
    for a in range(4):
        for h in range(hp):
            ret[a, slot * hp + h] = res[a, h, slot]
        for copy in back[a]:
            copy.wait_recv()
        for c in range(heads):
            cols = pl.ds(c * HD, HD)
            if a in (0, 3):
                outputs[a][:, :, cols] = (ret[a, c].astype(F32) + conv[a // 3, :, :, cols]).astype(BF16)
            else:
                outputs[a][:, :, cols] = ret[a, c]
    for copy in sent:
        copy.wait_send()
    for copy, sends, _ in edge_copies:
        pl.when(sends)(copy.wait_send)


def bias_rows(block_pairs, n, tokens):
    quarter = n // 4
    own = lax.axis_index("gx")
    rank = own % quarter
    blocks = tokens // BLOCK
    tiles = jnp.concatenate([
        rank + quarter * jnp.arange(4, dtype=jnp.int32),
        jnp.stack([(own + 1) % n, (own + n - 1) % n]).astype(jnp.int32),
    ])
    key_at = jnp.repeat(tiles, tokens) * blocks + jnp.tile(jnp.arange(tokens, dtype=jnp.int32) // BLOCK, 6)
    query = jnp.arange(8, dtype=jnp.int32)
    pairs = block_pairs[0, 0]
    listed = (pairs[:, 0][:, None, None] == query[None, :, None]) & (pairs[:, 1][:, None, None] == key_at[None, None, :])
    allowed = jnp.any(listed, axis=0) | ((own * blocks + query)[:, None] == key_at[None, :])
    return jnp.where(allowed, 0.0, NEG).astype(F32)


def per_device(n, m, queries, key_tokens, value_tokens, out_grad, conv_weight, block_pairs):
    tx, ty, width = queries.shape
    heads = width // HD
    hp = heads // 4
    tokens = tx * ty
    bias = bias_rows(block_pairs, n, tokens)
    vmem = pl.BlockSpec(memory_space=pltpu.VMEM)
    shape = jax.ShapeDtypeStruct(queries.shape, BF16)
    return pl.pallas_call(
        functools.partial(kernel, n, m, tx, ty),
        out_shape=(shape,) * 4,
        in_specs=[vmem] * 6,
        out_specs=(vmem,) * 4,
        scratch_shapes=[
            pltpu.VMEM((hp, 4, tx, ty, HD), BF16),
            pltpu.VMEM((hp, 4, tx, ty, HD), BF16),
            pltpu.VMEM((hp, 3, 4, tx, ty, HD), BF16),
            pltpu.VMEM((hp, 3, 4, tx, ty, HD), BF16),
            pltpu.VMEM((4, 8, 6 * tokens), F32),
            pltpu.VMEM((tokens, 6 * tokens), F32),
            pltpu.VMEM((hp, 4, tokens, HD), F32),
            pltpu.VMEM((hp, 4, tokens, HD), F32),
            pltpu.VMEM((2, hp, 2, 4, tx, ty, HD), BF16),
            pltpu.VMEM((2, hp, 2, 4, tx, ty, HD), BF16),
            pltpu.VMEM((4, hp, 4, tx, ty, HD), BF16),
            pltpu.VMEM((4, heads, tx, ty, HD), BF16),
            pltpu.VMEM((2, 2, ty, width), BF16),
            pltpu.VMEM((2, 2, tx + 2, 16, width), BF16),
            pltpu.VMEM((2, tx, ty, width), F32),
            pltpu.SemaphoreType.DMA((160,)),
            pltpu.SemaphoreType.DMA((160,)),
            pltpu.SemaphoreType.DMA((4 * hp + 1,)),
        ],
        compiler_params=pltpu.CompilerParams(
            collective_id=0, has_side_effects=True, vmem_limit_bytes=60 * 1024 * 1024
        ),
    )(queries, key_tokens, value_tokens, out_grad, conv_weight, bias)


def solution(mesh):
    grid = P("gx", "gy", None)
    return jax.shard_map(
        functools.partial(per_device, mesh.shape["gx"], mesh.shape["gy"]),
        mesh=mesh,
        in_specs=(grid, grid, grid, grid, P(), P("gx", "gy", None, None)),
        out_specs=(grid, grid, grid, grid),
        check_vma=False,
    )
```

profile of v0, /device:TPU:3, one launch (start us, length us, event | category | flops | bytes accessed | tf_op | source)
XLA Modules:
  0.0 120.3 jit_solution(15984031783679389143)
XLA Ops:
  0.7 0.1 add_multiply_fusion
  0.8 0.0 copy-start.3
  0.8 0.7 copy-done.3
  1.4 0.1 iota_compare_fusion
  1.5 0.1 broadcast_add_fusion
  1.6 0.1 broadcast_compare_fusion
  1.7 0.1 and_reduce_fusion
  1.8 0.7 or_select_fusion.bias_ref
  2.5 112.5 %shard_map.93 = (bf16[4,64,1024]{2,1,0:T(8,128)(2,1)}, bf16[4,64,1024]{2,1,0:T(8,128)(2,1)}, bf16[4,64,1024]{2,1,0:T(8,128)(2,1)}, bf16[4,64,1024]{2,1,0:T(8,128)(2,1)}) custom-call(bf16[4,64,1024]{2,1,0:T(8,128)(2,1)} %q_ref.1, bf16[4,64,1024]{2,1,0:T(8,128)(2,1)} %k_ref.1, bf16[4,64,1024]{2,1,0:T(8,128)(2,1)} %v_ref.1, bf16[4,64,1024]{2,1,0:T(8,128)(2,1)} %g_ref.1, ...), custom_call_target="tpu_custom_call" | custom-call | tf_op jit(solution)/shard_map/pallas_call | solution.py:333
  115.1 0.0 copy-start.2
  115.1 1.9 %copy.14 = bf16[4,64,1024]{2,1,0:T(8,128)(2,1)} copy(bf16[4,64,1024]{2,1,0:T(8,128)(2,1)} %get-tuple-element.10) | data formatting | bytes 1048576
  117.0 0.0 copy-done.2
  117.0 0.0 copy-start.1
  117.0 0.8 copy.15
  117.8 0.4 copy-done.1
  118.3 0.0 copy-start
  118.3 0.8 copy.16
  119.0 0.4 copy-done
  119.5 0.8 copy.17
  (5 shorter events, 0.0 us)
Async XLA Ops:
  0.8 0.7 copy-start.3
  115.1 1.9 %copy-start.2 = (bf16[4,64,1024]{2,1,0:T(8,128)(2,1)S(1)}, bf16[4,64,1024]{2,1,0:T(8,128)(2,1)}, u32[]{:S(2)}) copy-start(bf16[4,64,1024]{2,1,0:T(8,128)(2,1)} %get-tuple-element.11) | copy-start | bytes 1572868
  117.0 1.2 %copy-start.1 = (bf16[4,64,1024]{2,1,0:T(8,128)(2,1)S(1)}, bf16[4,64,1024]{2,1,0:T(8,128)(2,1)}, u32[]{:S(2)}) copy-start(bf16[4,64,1024]{2,1,0:T(8,128)(2,1)} %get-tuple-element.12) | copy-start | bytes 1572868
  118.3 1.2 %copy-start = (bf16[4,64,1024]{2,1,0:T(8,128)(2,1)S(1)}, bf16[4,64,1024]{2,1,0:T(8,128)(2,1)}, u32[]{:S(2)}) copy-start(bf16[4,64,1024]{2,1,0:T(8,128)(2,1)} %get-tuple-element.13) | copy-start | bytes 1572868
where the time goes:
time: 121 us; the launch traced here: 120 us
  Pallas kernels  113 us (93%)
  local copies, waits for them, and re-layouts  5.87 us (5%)
    pallas_call x1, Pallas kernels, per_device(): pl.pallas_call(functools.partial(kernel, n, m, tx, ty), out_shape=(shape,...  113 us
    unnamed x12, local copies, waits for them, and re-layouts  5.86 us

commit v1 on v0

v1 whole, which is shorter than its diff:
```python
import functools
import math

import jax
import jax.numpy as jnp
from jax import lax
from jax.experimental import pallas as pl
from jax.experimental.pallas import tpu as pltpu
from jax.sharding import PartitionSpec as P

HD = 128
BLOCK = 128
NEG = -1e30
MESH = pl.DeviceIdType.MESH
SCALE = 1.0 / math.sqrt(HD)
LOG2E = math.log2(math.e)
F32 = jnp.float32
BF16 = jnp.bfloat16
ORDER = (2, 3, 1)


def kernel(
    n, m, tx, ty,
    q_ref, k_ref, v_ref, g_ref, w_ref, pairs_ref,
    o_ref, dq_ref, dk_ref, dv_ref,
    qg, gg, kk, vv, bias_own, bias_g, s_sc, o_acc, dk_acc, dv_acc,
    part_send, part_recv, res, gedge, slab, w_sc, pairs_sc,
    send_sem, recv_sem, local_sem,
):
    tokens = tx * ty
    blocks = tokens // BLOCK
    heads = q_ref.shape[2] // HD
    hp = heads // 4
    quarter = n // 4
    own = lax.axis_index("gx")
    col = lax.axis_index("gy")
    slot = own // quarter
    rank = lax.rem(own, quarter)
    outputs = (o_ref, dq_ref, dk_ref, dv_ref)

    def far(d):
        return {"gx": lax.rem(own + d * quarter, n)}

    next_group = {"gx": slot * quarter + lax.rem(rank + 1, quarter)}
    prev_group = {"gx": slot * quarter + lax.rem(rank + quarter - 1, quarter)}
    groups = (next_group, prev_group)
    next_col = {"gy": lax.rem(col + 1, m)}
    prev_col = {"gy": lax.rem(col + m - 1, m)}
    cols_of = (next_col, prev_col)

    barrier = pltpu.get_barrier_semaphore()
    partners = [far(1), far(2), far(3), next_group, prev_group, next_col, prev_col]
    for partner in partners:
        pl.semaphore_signal(barrier, inc=1, device_id=partner, device_id_type=MESH)

    count = [0]
    sent = []
    local_count = [0]

    def reserve(k):
        at = count[0]
        count[0] += k
        return at

    def remote(src, dst, device, at):
        return pltpu.make_async_remote_copy(
            src_ref=src, dst_ref=dst, send_sem=send_sem.at[at], recv_sem=recv_sem.at[at],
            device_id=device, device_id_type=MESH,
        )

    def send(src, dst, device):
        copy = remote(src, dst, device, reserve(1))
        copy.start()
        sent.append(copy)
        return copy

    def local(src, dst):
        copy = pltpu.make_async_copy(src, dst, local_sem.at[local_count[0]])
        local_count[0] += 1
        copy.start()
        return copy

    def head_cols(head):
        return pl.ds(pl.multiple_of(head * HD, HD), HD)

    pairs_copy = local(pairs_ref, pairs_sc)
    w_copy = local(w_ref, w_sc)
    K, V, G, Q = 0, 1, 2, 3
    arrays = ((k_ref, lambda h, s: kk.at[h, 0, s]), (v_ref, lambda h, s: vv.at[h, 0, s]),
              (g_ref, lambda h, s: gg.at[h, s]), (q_ref, lambda h, s: qg.at[h, s]))
    mine = {}
    for h in range(hp):
        for a, (ref, place) in enumerate(arrays):
            mine[h, a] = local(ref.at[:, :, head_cols(slot * hp + h)], place(h, slot))

    pl.semaphore_wait(barrier, len(partners))

    incoming = {}
    in_base = {}
    for h in range(hp):
        for a, (ref, place) in enumerate(arrays):
            in_base[h, a] = count[0]
            for d in ORDER:
                target = lax.rem(slot + d, 4)
                incoming[h, a, d] = send(ref.at[:, :, head_cols(target * hp + h)], place(h, slot), far(d))

    forwards = {}
    fwd_base = {}
    bufs = (kk, vv)
    for h in range(hp):
        for a, (ref, _) in enumerate(arrays[:2]):
            for nb in (1, 2):
                forwards[h, a, 0, nb] = send(
                    ref.at[:, :, head_cols(slot * hp + h)], bufs[a].at[h, nb, slot], groups[2 - nb])
            fwd_base[h, a] = reserve(6)

    def order_at(t):
        return lax.rem(t + 1, 3) + 1

    def forward(h, a, t):
        s = lax.rem(slot + 4 - order_at(t), 4)
        remote(bufs[a].at[h, 0, s], bufs[a].at[h, 0, s], far(1), in_base[h, a] + t).wait_recv()
        for nb in (1, 2):
            remote(bufs[a].at[h, 0, s], bufs[a].at[h, nb, s], groups[2 - nb], fwd_base[h, a] + t * 2 + nb - 1).start()

    def forwards_done(h, a, recv):
        for nb in (1, 2):
            if recv:
                forwards[h, a, 0, nb].wait_recv()
            for t in range(3):
                copy = remote(bufs[a].at[h, 0, 0], bufs[a].at[h, nb, 0], groups[2 - nb], fwd_base[h, a] + t * 2 + nb - 1)
                if recv:
                    copy.wait_recv()
                else:
                    copy.wait_send()

    pairs_copy.wait()
    query_of = pairs_sc[0:1, :]
    key_of = pairs_sc[1:2, :]
    tiles = [rank + quarter * s for s in range(4)] + [lax.rem(own + 1, n), lax.rem(own + n - 1, n)]
    bias_own[...] = jnp.full(bias_own.shape, NEG, F32)
    for j, tile in enumerate(tiles):
        for c in range(blocks):
            key_id = tile * blocks + c
            for b in range(blocks):
                hit = jnp.where((query_of == b) & (key_of == key_id), 1.0, 0.0)
                hit = jnp.max(hit, axis=1, keepdims=True)
                hit = jnp.maximum(hit, (own * blocks + b == key_id).astype(F32))
                value = jnp.where(hit > 0.5, 0.0, NEG)
                at = j * tokens + c * BLOCK
                bias_own[b:b + 1, at:at + BLOCK] = jnp.broadcast_to(value, (1, BLOCK))
    bias_copies = [send(bias_own, bias_g.at[slot], far(d)) for d in ORDER]
    bias_mine = local(bias_own, bias_g.at[slot])
    w_copy.wait()

    ahead = (rank == quarter - 1).astype(jnp.int32)
    behind = 3 * (rank == 0).astype(jnp.int32)
    halo = {0: {}, 1: {}}
    edges = {}

    def halo_main(a, h):
        buf = vv.at[h, 0] if a == 0 else gg.at[h]
        halo[a][h] = [
            send(buf.at[:, :, pl.ds(first, 16)], slab.at[a, h, side, :, pl.ds(1, tx)], cols_of[side])
            for side, first in ((0, ty - 16), (1, 0))
        ]

    def halo_edges(a, h):
        for e, x in ((1, tx + 1), (2, 0)):
            if a == 0:
                row = vv.at[h, e, :, 0 if e == 1 else tx - 1]
            else:
                row = gedge.at[h, e - 1]
            for side, first in ((0, ty - 16), (1, 0)):
                halo[a][h].append(send(row.at[:, pl.ds(first, 16)], slab.at[a, h, side, :, x], cols_of[side]))

    def arrive_v(h):
        mine[h, V].wait()
        halo_main(0, h)

    def arrive_g(h):
        for d in ORDER:
            incoming[h, G, d].wait_recv()
        mine[h, G].wait()
        edges[h] = [send(gg.at[h, :, tx - 1], gedge.at[h, 1], next_group),
                    send(gg.at[h, :, 0], gedge.at[h, 0], prev_group)]
        halo_main(1, h)

    def arrive_rest(h):
        forwards_done(h, V, True)
        halo_edges(0, h)
        for d in ORDER:
            incoming[h, Q, d].wait_recv()
        for copy in edges[h]:
            copy.wait_recv()
        halo_edges(1, h)
        forwards_done(h, K, True)
        mine[h, K].wait()
        mine[h, Q].wait()

    has_left = (col > 0).astype(F32)
    has_right = (col < m - 1).astype(F32)

    def conv_tile(a, h, i):
        tile = i * quarter + rank
        has_up = (tile > 0).astype(F32)
        has_down = (tile < n - 1).astype(F32)
        above = lax.rem(i + behind, 4)
        below = lax.rem(i + ahead, 4)
        cols = head_cols(slot * hp + h)
        row_id = lax.broadcasted_iota(jnp.int32, (ty, HD), 0)
        sums = [None] * tx
        for x in range(tx + 2):
            if x == 0:
                row = (vv[h, 2, above, tx - 1] if a == 0 else gedge[h, 1, above]).astype(F32) * has_up
                at = above
            elif x == tx + 1:
                row = (vv[h, 1, below, 0] if a == 0 else gedge[h, 0, below]).astype(F32) * has_down
                at = below
            else:
                row = (vv[h, 0, i, x - 1] if a == 0 else gg[h, i, x - 1]).astype(F32)
                at = i
            left = slab[a, h, 0, at, x].astype(F32)[15:16] * has_left
            right = slab[a, h, 1, at, x].astype(F32)[0:1] * has_right
            if x == 0:
                left, right = left * has_up, right * has_up
            if x == tx + 1:
                left, right = left * has_down, right * has_down
            shifted = (
                jnp.where(row_id == 0, left, pltpu.roll(row, 1, 0)),
                row,
                jnp.where(row_id == ty - 1, right, pltpu.roll(row, ty - 1, 0)),
            )
            for step in (-1, 0, 1):
                target = x - 1 - step
                if 0 <= target < tx:
                    for b in range(3):
                        tap = 3 * (step + 1) + b
                        tap = tap if a == 0 else 8 - tap
                        term = w_sc[pl.ds(tap, 1), cols] * shifted[b]
                        sums[target] = term if sums[target] is None else sums[target] + term
        return jnp.concatenate(sums, axis=0)

    nt = (((1,), (1,)), ((), ()))
    nn = (((1,), (0,)), ((), ()))
    tn = (((0,), (0,)), ((), ()))

    def dot(x, y, dims):
        return lax.dot_general(x, y, dims, preferred_element_type=F32)

    def flat(x):
        return x.reshape(tokens, HD)

    back_base = {}

    def give_back(a, h, t, i):
        cols = head_cols(slot * hp + h)

        @pl.when(t < 3)
        def _():
            remote(res.at[a, h, i], outputs[a].at[:, :, cols], {"gx": i * quarter + rank}, back_base[a, h] + t).start()

    def keep(a, h):
        return local(res.at[a, h, slot], outputs[a].at[:, :, head_cols(slot * hp + h)])

    part_base = {}

    def attend(h):
        back_base[1, h] = reserve(3)
        part_base[h] = reserve(16)
        dk_acc[...] = jnp.zeros(dk_acc.shape, F32)
        dv_acc[...] = jnp.zeros(dv_acc.shape, F32)

        @pl.loop(0, 4)
        def _(t):
            i = lax.rem(slot + lax.rem(t + 1, 3) + 1, 4)
            i = lax.select(t == 3, slot, i)
            q = flat(qg[h, i])
            g = flat(gg[h, i])
            keys = [(0, 0), (0, 1), (0, 2), (0, 3), (1, lax.rem(i + ahead, 4)), (2, lax.rem(i + behind, 4))]
            top = None
            for j, (nb, s) in enumerate(keys):
                js = pl.ds(j * tokens, tokens)
                score = dot(q, flat(kk[h, nb, s]), nt)
                bias = bias_g[i, :, js]
                parts = [score[b * BLOCK:(b + 1) * BLOCK] + bias[b:b + 1] for b in range(blocks)]
                score = jnp.concatenate(parts, axis=0)
                s_sc[:, js] = score
                peak = jnp.max(score, axis=1, keepdims=True)
                top = peak if top is None else jnp.maximum(top, peak)
            total = jnp.zeros((tokens, 1), F32)
            out = jnp.zeros((tokens, HD), F32)
            for j, (nb, s) in enumerate(keys):
                js = pl.ds(j * tokens, tokens)
                prob = jnp.exp2((s_sc[:, js] - top) * (SCALE * LOG2E))
                s_sc[:, js] = prob
                total = total + jnp.sum(prob, axis=1, keepdims=True)
                out = out + dot(prob.astype(BF16), flat(vv[h, nb, s]), nn)
            inv = 1.0 / total
            out = out * inv
            o_acc[i] = out
            grad_dot = jnp.sum(g.astype(F32) * out, axis=1, keepdims=True)
            dq = jnp.zeros((tokens, HD), F32)
            for j, (nb, s) in enumerate(keys):
                js = pl.ds(j * tokens, tokens)
                prob_grad = dot(g, flat(vv[h, nb, s]), nt)
                prob = s_sc[:, js] * inv
                score_grad = (prob * (prob_grad - grad_dot)).astype(BF16)
                dq = dq + dot(score_grad, flat(kk[h, nb, s]), nn)
                dk = dot(score_grad, q, tn)
                dv = dot(prob.astype(BF16), g, tn)
                if nb == 0:
                    dk_acc[s] += dk
                    dv_acc[s] += dv
                else:
                    for a, value in enumerate((dk, dv)):
                        part_send[a, h, nb - 1, s] = value.astype(BF16).reshape(tx, ty, HD)
                        remote(part_send.at[a, h, nb - 1, s], part_recv.at[a, h, nb - 1, s], groups[nb - 1],
                               part_base[h] + t * 4 + a * 2 + nb - 1).start()
            res[1, h, i] = (dq * SCALE).astype(BF16).reshape(tx, ty, HD)
            give_back(1, h, t, i)
            if h + 1 < hp:

                @pl.when(t < 3)
                def _():
                    forward(h + 1, K, t)
                    forward(h + 1, V, t)

        kept.append(keep(1, h))

    def tile_at(t):
        return lax.select(t == 3, slot, lax.rem(slot + lax.rem(t + 1, 3) + 1, 4))

    def finish_out(h):
        for copy in halo[0][h]:
            copy.wait_recv()
        back_base[0, h] = reserve(3)

        @pl.loop(0, 4)
        def _(t):
            i = tile_at(t)
            res[0, h, i] = (o_acc[i] + conv_tile(0, h, i)).astype(BF16).reshape(tx, ty, HD)
            give_back(0, h, t, i)

        kept.append(keep(0, h))

    def part_copy(h, t, a, nb):
        return remote(part_send.at[a, h, nb, 0], part_recv.at[a, h, nb, 0], groups[nb], part_base[h] + t * 4 + a * 2 + nb)

    def finish_grads(h):
        for t in range(4):
            for a in range(2):
                for nb in range(2):
                    part_copy(h, t, a, nb).wait_recv()
        for copy in halo[1][h]:
            copy.wait_recv()
        back_base[2, h] = reserve(3)
        back_base[3, h] = reserve(3)

        @pl.loop(0, 4)
        def _(t):
            s = tile_at(t)
            for a, acc in enumerate((dk_acc, dv_acc)):
                value = acc[s] + flat(part_recv[a, h, 0, s]).astype(F32) + flat(part_recv[a, h, 1, s]).astype(F32)
                value = value * SCALE if a == 0 else value + conv_tile(1, h, s)
                res[2 + a, h, s] = value.astype(BF16).reshape(tx, ty, HD)
                give_back(2 + a, h, t, s)

        kept.append(keep(2, h))
        kept.append(keep(3, h))

    kept = []
    for t in range(3):
        forward(0, K, t)
    for t in range(3):
        forward(0, V, t)
    for h in range(hp):
        arrive_v(h)
        arrive_g(h)
        arrive_rest(h)
        if h == 0:
            bias_mine.wait()
            for copy in bias_copies:
                copy.wait_recv()
        attend(h)
        finish_out(h)
        finish_grads(h)

    for copy in kept:
        copy.wait()
    for a in range(4):
        for h in range(hp):
            for t in range(3):
                copy = remote(res.at[a, h, 0], outputs[a].at[:, :, head_cols(slot * hp + h)], far(1), back_base[a, h] + t)
                copy.wait_recv()
                copy.wait_send()
    for h in range(hp):
        for a in range(2):
            forwards_done(h, a, False)
            for t in range(4):
                for nb in range(2):
                    part_copy(h, t, a, nb).wait_send()
    for copy in sent:
        copy.wait_send()


def hand_over(*refs):
    count = (len(refs) - 2) // 2
    sources, targets = refs[:count], refs[count:2 * count]
    stage, sems = refs[2 * count:]
    first = [pltpu.make_async_copy(sources[a], stage.at[a], sems.at[0, a]) for a in range(count)]
    second = [pltpu.make_async_copy(stage.at[a], targets[a], sems.at[1, a]) for a in range(count)]
    for copy in first:
        copy.start()
    for a in range(count):
        first[a].wait()
        second[a].start()
    for copy in second:
        copy.wait()


def per_device(n, m, queries, key_tokens, value_tokens, out_grad, conv_weight, block_pairs):
    tx, ty, width = queries.shape
    heads = width // HD
    hp = heads // 4
    tokens = tx * ty
    pairs = block_pairs.shape[2]
    vmem = pl.BlockSpec(memory_space=pltpu.VMEM)
    anywhere = pl.BlockSpec(memory_space=pl.ANY)
    shape = jax.ShapeDtypeStruct(queries.shape, BF16)
    outs = pl.pallas_call(
        functools.partial(kernel, n, m, tx, ty),
        out_shape=(shape,) * 4,
        in_specs=[anywhere] * 6,
        out_specs=(anywhere,) * 4,
        scratch_shapes=[
            pltpu.VMEM((hp, 4, tx, ty, HD), BF16),
            pltpu.VMEM((hp, 4, tx, ty, HD), BF16),
            pltpu.VMEM((hp, 3, 4, tx, ty, HD), BF16),
            pltpu.VMEM((hp, 3, 4, tx, ty, HD), BF16),
            pltpu.VMEM((8, 6 * tokens), F32),
            pltpu.VMEM((4, 8, 6 * tokens), F32),
            pltpu.VMEM((tokens, 6 * tokens), F32),
            pltpu.VMEM((4, tokens, HD), F32),
            pltpu.VMEM((4, tokens, HD), F32),
            pltpu.VMEM((4, tokens, HD), F32),
            pltpu.VMEM((2, hp, 2, 4, tx, ty, HD), BF16),
            pltpu.VMEM((2, hp, 2, 4, tx, ty, HD), BF16),
            pltpu.VMEM((4, hp, 4, tx, ty, HD), BF16),
            pltpu.VMEM((hp, 2, 4, ty, HD), BF16),
            pltpu.VMEM((2, hp, 2, 4, tx + 2, 16, HD), BF16),
            pltpu.VMEM((9, width), F32),
            pltpu.VMEM((2, pairs), jnp.int32),
            pltpu.SemaphoreType.DMA((160,)),
            pltpu.SemaphoreType.DMA((160,)),
            pltpu.SemaphoreType.DMA((8 * hp + 3,)),
        ],
        compiler_params=pltpu.CompilerParams(
            collective_id=0, has_side_effects=True, vmem_limit_bytes=60 * 1024 * 1024
        ),
    )(queries, key_tokens, value_tokens, out_grad, conv_weight, block_pairs[0, 0].T)
    return pl.pallas_call(
        hand_over,
        out_shape=(shape,) * 4,
        in_specs=[anywhere] * 4,
        out_specs=(anywhere,) * 4,
        scratch_shapes=[pltpu.VMEM((4, tx, ty, width), BF16), pltpu.SemaphoreType.DMA((2, 4))],
    )(*outs)


def solution(mesh):
    grid = P("gx", "gy", None)
    return jax.shard_map(
        functools.partial(per_device, mesh.shape["gx"], mesh.shape["gy"]),
        mesh=mesh,
        in_specs=(grid, grid, grid, grid, P(), P("gx", "gy", None, None)),
        out_specs=(grid, grid, grid, grid),
        check_vma=False,
    )
```

time: 121 us -> 117 us (0.967)
  the two profiles are of different devices: /device:TPU:3 before, /device:TPU:9 now
where the time goes in v1:
time: 117 us; the launch traced here: 116 us
  Pallas kernels  116 us (99%)
    pallas_call x1, Pallas kernels, per_device(): pl.pallas_call(functools.partial(kernel, n, m, tx, ty), out_shape=(shape,...  113 us
    pallas_call x1, Pallas kernels, per_device(): pl.pallas_call(hand_over, out_shape=(shape,) * 4, in_specs=[anywhere] * 4...  2.42 us

profile of v1, /device:TPU:9, one launch (start us, length us, event | category | flops | bytes accessed | tf_op | source)
XLA Modules:
  0.0 116.4 jit_solution(8900220231556628620)
XLA Ops:
  0.6 113.3 %shard_map.93 = (bf16[4,64,1024]{2,1,0:T(8,128)(2,1)}, bf16[4,64,1024]{2,1,0:T(8,128)(2,1)}, bf16[4,64,1024]{2,1,0:T(8,128)(2,1)}, bf16[4,64,1024]{2,1,0:T(8,128)(2,1)}) custom-call(bf16[4,64,1024]{2,1,0:T(8,128)(2,1)} %q_ref.1, bf16[4,64,1024]{2,1,0:T(8,128)(2,1)} %k_ref.1, bf16[4,64,1024]{2,1,0:T(8,128)(2,1)} %v_ref.1, bf16[4,64,1024]{2,1,0:T(8,128)(2,1)} %g_ref.1, ...), custom_call_target="tpu_custom_call" | custom-call | tf_op jit(solution)/shard_map/pallas_call | solution.py:431
  114.0 2.4 %shard_map.94 = (bf16[4,64,1024]{2,1,0:T(8,128)(2,1)}, bf16[4,64,1024]{2,1,0:T(8,128)(2,1)}, bf16[4,64,1024]{2,1,0:T(8,128)(2,1)}, bf16[4,64,1024]{2,1,0:T(8,128)(2,1)}) custom-call(bf16[4,64,1024]{2,1,0:T(8,128)(2,1)} %get-tuple-element.8.refs_0_, bf16[4,64,1024]{2,1,0:T(8,128)(2,1)} %get-tuple-element.9.refs_1_, ...), custom_call_target="tpu_custom_call" | custom-call | tf_op jit(solution)/shard_map/pallas_call | solution.py:462

commit v2 on v1

--- a/solution.py
+++ b/solution.py
@@ -23,7 +23,7 @@
     n, m, tx, ty,
     q_ref, k_ref, v_ref, g_ref, w_ref, pairs_ref,
     o_ref, dq_ref, dk_ref, dv_ref,
-    qg, gg, kk, vv, bias_own, bias_g, s_sc, o_acc, dk_acc, dv_acc,
+    qg, gg, kk, vv, bias_g, s_sc, o_acc, dk_acc, dv_acc,
     part_send, part_recv, res, gedge, slab, w_sc, pairs_sc,
     send_sem, recv_sem, local_sem,
 ):
@@ -83,7 +83,7 @@
     def head_cols(head):
         return pl.ds(pl.multiple_of(head * HD, HD), HD)
 
-    pairs_copy = local(pairs_ref, pairs_sc)
+    pairs_copy = local(pairs_ref, pairs_sc.at[slot])
     w_copy = local(w_ref, w_sc)
     K, V, G, Q = 0, 1, 2, 3
     arrays = ((k_ref, lambda h, s: kk.at[h, 0, s]), (v_ref, lambda h, s: vv.at[h, 0, s]),
@@ -95,6 +95,7 @@
 
     pl.semaphore_wait(barrier, len(partners))
 
+    pairs_copies = [send(pairs_ref, pairs_sc.at[slot], far(d)) for d in ORDER]
     incoming = {}
     in_base = {}
     for h in range(hp):
@@ -134,23 +135,26 @@
                 else:
                     copy.wait_send()
 
-    pairs_copy.wait()
-    query_of = pairs_sc[0:1, :]
-    key_of = pairs_sc[1:2, :]
-    tiles = [rank + quarter * s for s in range(4)] + [lax.rem(own + 1, n), lax.rem(own + n - 1, n)]
-    bias_own[...] = jnp.full(bias_own.shape, NEG, F32)
-    for j, tile in enumerate(tiles):
-        for c in range(blocks):
-            key_id = tile * blocks + c
-            for b in range(blocks):
-                hit = jnp.where((query_of == b) & (key_of == key_id), 1.0, 0.0)
-                hit = jnp.max(hit, axis=1, keepdims=True)
-                hit = jnp.maximum(hit, (own * blocks + b == key_id).astype(F32))
-                value = jnp.where(hit > 0.5, 0.0, NEG)
-                at = j * tokens + c * BLOCK
-                bias_own[b:b + 1, at:at + BLOCK] = jnp.broadcast_to(value, (1, BLOCK))
-    bias_copies = [send(bias_own, bias_g.at[slot], far(d)) for d in ORDER]
-    bias_mine = local(bias_own, bias_g.at[slot])
+    def make_bias():
+        bias_g[...] = jnp.full(bias_g.shape, NEG, F32)
+
+        @pl.loop(0, 4)
+        def _(i):
+            tile = i * quarter + rank
+            query_of = pairs_sc[i, 0:1, :]
+            key_of = pairs_sc[i, 1:2, :]
+            near = [rank + quarter * s for s in range(4)] + [lax.rem(tile + 1, n), lax.rem(tile + n - 1, n)]
+            for j, key_tile in enumerate(near):
+                for c in range(blocks):
+                    key_id = key_tile * blocks + c
+                    for b in range(blocks):
+                        hit = jnp.where((query_of == b) & (key_of == key_id), 1.0, 0.0)
+                        hit = jnp.max(hit, axis=1, keepdims=True)
+                        hit = jnp.maximum(hit, (tile * blocks + b == key_id).astype(F32))
+                        value = jnp.where(hit > 0.5, 0.0, NEG)
+                        at = j * tokens + c * BLOCK
+                        bias_g[i, b:b + 1, at:at + BLOCK] = jnp.broadcast_to(value, (1, BLOCK))
+
     w_copy.wait()
 
     ahead = (rank == quarter - 1).astype(jnp.int32)
@@ -370,6 +374,10 @@
         kept.append(keep(3, h))
 
     kept = []
+    pairs_copy.wait()
+    for copy in pairs_copies:
+        copy.wait_recv()
+    make_bias()
     for t in range(3):
         forward(0, K, t)
     for t in range(3):
@@ -378,10 +386,6 @@
         arrive_v(h)
         arrive_g(h)
         arrive_rest(h)
-        if h == 0:
-            bias_mine.wait()
-            for copy in bias_copies:
-                copy.wait_recv()
         attend(h)
         finish_out(h)
         finish_grads(h)
@@ -438,7 +442,6 @@
             pltpu.VMEM((hp, 4, tx, ty, HD), BF16),
             pltpu.VMEM((hp, 3, 4, tx, ty, HD), BF16),
             pltpu.VMEM((hp, 3, 4, tx, ty, HD), BF16),
-            pltpu.VMEM((8, 6 * tokens), F32),
             pltpu.VMEM((4, 8, 6 * tokens), F32),
             pltpu.VMEM((tokens, 6 * tokens), F32),
             pltpu.VMEM((4, tokens, HD), F32),
@@ -450,10 +453,10 @@
             pltpu.VMEM((hp, 2, 4, ty, HD), BF16),
             pltpu.VMEM((2, hp, 2, 4, tx + 2, 16, HD), BF16),
             pltpu.VMEM((9, width), F32),
-            pltpu.VMEM((2, pairs), jnp.int32),
+            pltpu.VMEM((4, 2, pairs), jnp.int32),
             pltpu.SemaphoreType.DMA((160,)),
             pltpu.SemaphoreType.DMA((160,)),
-            pltpu.SemaphoreType.DMA((8 * hp + 3,)),
+            pltpu.SemaphoreType.DMA((8 * hp + 2,)),
         ],
         compiler_params=pltpu.CompilerParams(
             collective_id=0, has_side_effects=True, vmem_limit_bytes=60 * 1024 * 1024

time: 117 us -> 101 us (0.86)
  Pallas kernels: 116 us -> 100 us
    pallas_call x1, Pallas kernels: 113 us -> 97.9 us  [per_device(): pl.pallas_call(functools.partial(kernel, n, m, tx, ty), out_shape=(shape,...]
where the time goes in v2:
time: 101 us
  Pallas kernels  100 us (99%)
    pallas_call x1, Pallas kernels, per_device(): pl.pallas_call(functools.partial(kernel, n, m, tx, ty), out_shape=(shape,...  97.9 us
    pallas_call x1, Pallas kernels, per_device(): pl.pallas_call(hand_over, out_shape=(shape,) * 4, in_specs=[anywhere] * 4...  2.42 us

profile of v2, /device:TPU:9, one launch (start us, length us, event | category | flops | bytes accessed | tf_op | source)
XLA Modules:
  0.0 100.9 jit_solution(1515743465260676214)
XLA Ops:
  0.6 97.9 %shard_map.93 = (bf16[4,64,1024]{2,1,0:T(8,128)(2,1)}, bf16[4,64,1024]{2,1,0:T(8,128)(2,1)}, bf16[4,64,1024]{2,1,0:T(8,128)(2,1)}, bf16[4,64,1024]{2,1,0:T(8,128)(2,1)}) custom-call(bf16[4,64,1024]{2,1,0:T(8,128)(2,1)} %q_ref.1, bf16[4,64,1024]{2,1,0:T(8,128)(2,1)} %k_ref.1, bf16[4,64,1024]{2,1,0:T(8,128)(2,1)} %v_ref.1, bf16[4,64,1024]{2,1,0:T(8,128)(2,1)} %g_ref.1, ...), custom_call_target="tpu_custom_call" | custom-call | tf_op jit(solution)/shard_map/pallas_call | solution.py:435
  98.5 2.4 %shard_map.94 = (bf16[4,64,1024]{2,1,0:T(8,128)(2,1)}, bf16[4,64,1024]{2,1,0:T(8,128)(2,1)}, bf16[4,64,1024]{2,1,0:T(8,128)(2,1)}, bf16[4,64,1024]{2,1,0:T(8,128)(2,1)}) custom-call(bf16[4,64,1024]{2,1,0:T(8,128)(2,1)} %get-tuple-element.8.refs_0_, bf16[4,64,1024]{2,1,0:T(8,128)(2,1)} %get-tuple-element.9.refs_1_, ...), custom_call_target="tpu_custom_call" | custom-call | tf_op jit(solution)/shard_map/pallas_call | solution.py:465

commit v3 on v2

--- a/solution.py
+++ b/solution.py
@@ -409,17 +409,12 @@
 
 
 def hand_over(*refs):
-    count = (len(refs) - 2) // 2
-    sources, targets = refs[:count], refs[count:2 * count]
-    stage, sems = refs[2 * count:]
-    first = [pltpu.make_async_copy(sources[a], stage.at[a], sems.at[0, a]) for a in range(count)]
-    second = [pltpu.make_async_copy(stage.at[a], targets[a], sems.at[1, a]) for a in range(count)]
-    for copy in first:
+    count = (len(refs) - 1) // 2
+    sources, targets, sems = refs[:count], refs[count:2 * count], refs[-1]
+    copies = [pltpu.make_async_copy(sources[a], targets[a], sems.at[a]) for a in range(count)]
+    for copy in copies:
         copy.start()
-    for a in range(count):
-        first[a].wait()
-        second[a].start()
-    for copy in second:
+    for copy in copies:
         copy.wait()
 
 
@@ -434,9 +429,9 @@
     shape = jax.ShapeDtypeStruct(queries.shape, BF16)
     outs = pl.pallas_call(
         functools.partial(kernel, n, m, tx, ty),
-        out_shape=(shape,) * 4,
+        out_shape=(pltpu.VMEM(queries.shape, BF16),) * 4,
         in_specs=[anywhere] * 6,
-        out_specs=(anywhere,) * 4,
+        out_specs=(vmem,) * 4,
         scratch_shapes=[
             pltpu.VMEM((hp, 4, tx, ty, HD), BF16),
             pltpu.VMEM((hp, 4, tx, ty, HD), BF16),
@@ -459,15 +454,16 @@
             pltpu.SemaphoreType.DMA((8 * hp + 2,)),
         ],
         compiler_params=pltpu.CompilerParams(
-            collective_id=0, has_side_effects=True, vmem_limit_bytes=60 * 1024 * 1024
+            collective_id=0, has_side_effects=True, vmem_limit_bytes=64500000
         ),
     )(queries, key_tokens, value_tokens, out_grad, conv_weight, block_pairs[0, 0].T)
     return pl.pallas_call(
         hand_over,
         out_shape=(shape,) * 4,
-        in_specs=[anywhere] * 4,
+        in_specs=[vmem] * 4,
         out_specs=(anywhere,) * 4,
-        scratch_shapes=[pltpu.VMEM((4, tx, ty, width), BF16), pltpu.SemaphoreType.DMA((2, 4))],
+        scratch_shapes=[pltpu.SemaphoreType.DMA((4,))],
+        compiler_params=pltpu.CompilerParams(vmem_limit_bytes=4 * 1024 * 1024),
     )(*outs)
 
 

time: 101 us -> 100 us (0.990)
    pallas_call x2, Pallas kernels: 100 us -> 99.2 us  [the longest x1 97.8 us: per_device(): pl.pallas_call(functools.partial(kernel, n, m, tx, ty), out_shape=(pltpu....]
where the time goes in v3:
time: 100 us; the launch traced here: 99.8 us
  Pallas kernels  99.2 us (99%)
    pallas_call x1, Pallas kernels, per_device(): pl.pallas_call(functools.partial(kernel, n, m, tx, ty), out_shape=(pltpu....  97.8 us

profile of v3, /device:TPU:9, one launch (start us, length us, event | category | flops | bytes accessed | tf_op | source)
XLA Modules:
  0.0 99.8 jit_solution(2021657880282716564)
XLA Ops:
  0.6 97.8 %shard_map.93 = (bf16[4,64,1024]{2,1,0:T(8,128)(2,1)S(1)}, bf16[4,64,1024]{2,1,0:T(8,128)(2,1)S(1)}, bf16[4,64,1024]{2,1,0:T(8,128)(2,1)S(1)}, bf16[4,64,1024]{2,1,0:T(8,128)(2,1)S(1)}) custom-call(bf16[4,64,1024]{2,1,0:T(8,128)(2,1)} %q_ref.1, bf16[4,64,1024]{2,1,0:T(8,128)(2,1)} %k_ref.1, bf16[4,64,1024]{2,1,0:T(8,128)(2,1)} %v_ref.1, ...), custom_call_target="tpu_custom_call" | custom-call | tf_op jit(solution)/shard_map/pallas_call | solution.py:430
  98.5 1.3 %shard_map.94 = (bf16[4,64,1024]{2,1,0:T(8,128)(2,1)}, bf16[4,64,1024]{2,1,0:T(8,128)(2,1)}, bf16[4,64,1024]{2,1,0:T(8,128)(2,1)}, bf16[4,64,1024]{2,1,0:T(8,128)(2,1)}) custom-call(bf16[4,64,1024]{2,1,0:T(8,128)(2,1)S(1)} %get-tuple-element.8.refs_0_, bf16[4,64,1024]{2,1,0:T(8,128)(2,1)S(1)} %get-tuple-element.9.refs_1_, ...), custom_call_target="tpu_custom_call" | custom-call | tf_op jit(solution)/shard_map/pallas_call | solution.py:460
